TPU v7x, 32 devices: a whole 2x2x4 slice. The times are simulated.
32 devices in a mesh: dp: 16 (over z, x, core), tensor: 2 (over y).
Axes of the slice: x: 2, y: 2, z: 4, core: 2. Of those that a mesh axis runs over, the one named last changes fastest.
Arguments:
- x_input: bfloat16 [16, 768, 1536], P('dp', 'tensor'), may hold values from -6 to 6
- cond_tokens: bfloat16 [16, 130, 1536], P('dp'), may hold values from -6 to 6
- teacher: bfloat16 [16, 768, 1536], P('dp', 'tensor'), may hold values from -6 to 6
- valid_mask: int32 [16, 768], P('dp', 'tensor'), may hold values from 0 to 1, as said below
- norm_gains: bfloat16 [3, 1536], P(None, 'dp'), may hold values from 0.099609375 to 1.8984375
- w_query: bfloat16 [1536, 1536], P('dp', 'tensor'), may hold values from -0.15625 to 0.15625
- w_key: bfloat16 [1536, 1536], P('dp', 'tensor'), may hold values from -0.15625 to 0.15625
- w_value: bfloat16 [1536, 1536], P('dp', 'tensor'), may hold values from -0.15625 to 0.15625
- w_out: bfloat16 [1536, 1536], P('tensor', 'dp'), may hold values from -3 to 3
- c_query: bfloat16 [1536, 1536], P('dp', 'tensor'), may hold values from -0.15625 to 0.15625
- c_key: bfloat16 [1536, 1536], P('dp', 'tensor'), may hold values from -0.15625 to 0.15625
- c_value: bfloat16 [1536, 1536], P('dp', 'tensor'), may hold values from -0.15625 to 0.15625
- c_out: bfloat16 [1536, 1536], P('tensor', 'dp'), may hold values from -1.25 to 1.25
- w_gate: bfloat16 [1536, 6144], P('dp', 'tensor'), may hold values from -0.15625 to 0.15625
- w_up: bfloat16 [1536, 6144], P('dp', 'tensor'), may hold values from -0.15625 to 0.15625
- w_down: bfloat16 [6144, 1536], P('tensor', 'dp'), may hold values from -0.078125 to 0.078125
Outputs:
- output: bfloat16 [16, 768, 1536], P('dp', 'tensor')
- mean_loss: float32 [], replicated
- grad_input: float32 [16, 768, 1536], P('dp', 'tensor')
- grad_cond: float32 [16, 130, 1536], P('dp')
- grad_w_query: float32 [1536, 1536], P('dp', 'tensor')
- grad_w_key: float32 [1536, 1536], P('dp', 'tensor')
- grad_w_value: float32 [1536, 1536], P('dp', 'tensor')
- grad_w_out: float32 [1536, 1536], P('tensor', 'dp')
- grad_c_query: float32 [1536, 1536], P('dp', 'tensor')
- grad_c_key: float32 [1536, 1536], P('dp', 'tensor')
- grad_c_value: float32 [1536, 1536], P('dp', 'tensor')
- grad_c_out: float32 [1536, 1536], P('tensor', 'dp')
- grad_w_gate: float32 [1536, 6144], P('dp', 'tensor')
- grad_w_up: float32 [1536, 6144], P('dp', 'tensor')
- grad_w_down: float32 [6144, 1536], P('tensor', 'dp')
- grad_norm_gains: float32 [3, 1536], P(None, 'dp')
Inputs may be any that keep to these rules, and one draw needn't show every extreme that they name: `valid_mask`: the valid tokens of each latent form a prefix of it, and every latent has a valid token.
All inputs are finite; a program needn't handle non-finite values.
Results may differ from a plain program's by a relative error of at most 0.017.
Values may be sent and summed in bfloat16 or wider, within the bound.
No kernel may reach another device: no remote copies, remote signals or barrier semaphores. Data moves between devices by JAX's collectives and lax.ppermute only.
A program may use at most 256 MiB of HBM per device.

v0:
```python
import math
import jax
import jax.numpy as jnp
from jax import lax
from jax.sharding import PartitionSpec as P

HEAD_DIM = 64
EPSILON = 1e-05


def matmul(left_side, right_side):
    return jnp.dot(left_side, right_side, preferred_element_type=jnp.float32)


def contract_rows(left_side, right_side):
    return lax.dot_general(
        left_side, right_side, (((0,), (0,)), ((), ())), preferred_element_type=jnp.float32
    )


def times_transposed(left_side, right_side):
    return lax.dot_general(
        left_side, right_side, (((1,), (1,)), ((), ())), preferred_element_type=jnp.float32
    )


def norm_stats(values):
    row_mean = jnp.mean(values, axis=-1, keepdims=True)
    centred = values - row_mean
    row_var = jnp.mean(centred * centred, axis=-1, keepdims=True)
    inverse = lax.rsqrt(row_var + EPSILON)
    return (centred * inverse, inverse)


def norm_back(grad_normed, normed, inverse, gain_row):
    scaled = grad_normed * gain_row
    mean_scaled = jnp.mean(scaled, axis=-1, keepdims=True)
    mean_product = jnp.mean(scaled * normed, axis=-1, keepdims=True)
    grad_values = inverse * (scaled - mean_scaled - normed * mean_product)
    return (grad_values, jnp.sum(grad_normed * normed, axis=0))


def rotary_tables(length):
    half_dim = HEAD_DIM // 2
    freqs = jnp.exp(jnp.arange(half_dim, dtype=jnp.float32) * (-math.log(10000.0) / half_dim))
    angles = jnp.arange(length, dtype=jnp.float32)[:, None] * freqs[None, :]
    return (jnp.cos(angles)[:, None, :], jnp.sin(angles)[:, None, :])


def rotate(values, rot_cos, rot_sin):
    half_dim = HEAD_DIM // 2
    lower = values[..., :half_dim]
    upper = values[..., half_dim:]
    return jnp.concatenate(
        [lower * rot_cos - upper * rot_sin, upper * rot_cos + lower * rot_sin], axis=-1
    )


def rotate_back(values, rot_cos, rot_sin):
    half_dim = HEAD_DIM // 2
    lower = values[..., :half_dim]
    upper = values[..., half_dim:]
    return jnp.concatenate(
        [lower * rot_cos + upper * rot_sin, upper * rot_cos - lower * rot_sin], axis=-1
    )


def attend_forward(queries, keys_in, values_in):
    scale_factor = HEAD_DIM ** (-0.5)
    scores = (
        jnp.einsum("qhd,khd->hqk", queries, keys_in, preferred_element_type=jnp.float32)
        * scale_factor
    )
    row_max = jnp.max(scores, axis=-1, keepdims=True)
    shifted = jnp.exp(scores - row_max)
    row_total = jnp.sum(shifted, axis=-1, keepdims=True)
    soft_probs = (shifted / row_total).astype(jnp.bfloat16)
    mixed = jnp.einsum("hqk,khd->qhd", soft_probs, values_in, preferred_element_type=jnp.float32)
    return (mixed, row_max + jnp.log(row_total))


def attend_back(queries, keys_in, values_in, log_total, grad_mixed):
    scale_factor = HEAD_DIM ** (-0.5)
    scores = (
        jnp.einsum("qhd,khd->hqk", queries, keys_in, preferred_element_type=jnp.float32)
        * scale_factor
    )
    soft_probs = jnp.exp(scores - log_total)
    grad_values = jnp.einsum(
        "hqk,qhd->khd",
        soft_probs.astype(jnp.bfloat16),
        grad_mixed,
        preferred_element_type=jnp.float32,
    )
    grad_probs = jnp.einsum(
        "qhd,khd->hqk", grad_mixed, values_in, preferred_element_type=jnp.float32
    )
    weighted = jnp.sum(soft_probs * grad_probs, axis=-1, keepdims=True)
    grad_scores = (soft_probs * (grad_probs - weighted)).astype(jnp.bfloat16)
    grad_queries = (
        jnp.einsum("hqk,khd->qhd", grad_scores, keys_in, preferred_element_type=jnp.float32)
        * scale_factor
    )
    grad_keys = (
        jnp.einsum("hqk,qhd->khd", grad_scores, queries, preferred_element_type=jnp.float32)
        * scale_factor
    )
    return (grad_queries, grad_keys, grad_values)


def body(
    x_input,
    cond_tokens,
    teacher,
    valid_mask,
    norm_gains,
    w_query,
    w_key,
    w_value,
    w_out,
    c_query,
    c_key,
    c_value,
    c_out,
    w_gate,
    w_up,
    w_down,
):
    bf_type = jnp.bfloat16

    def fetch_attention():
        return (
            lax.all_gather(w_query, "dp", axis=0, tiled=True),
            lax.all_gather(w_key, "dp", axis=0, tiled=True),
            lax.all_gather(w_value, "dp", axis=0, tiled=True),
            lax.all_gather(w_out, "dp", axis=1, tiled=True),
            lax.all_gather(c_query, "dp", axis=0, tiled=True),
            lax.all_gather(c_key, "dp", axis=0, tiled=True),
            lax.all_gather(c_value, "dp", axis=0, tiled=True),
            lax.all_gather(c_out, "dp", axis=1, tiled=True),
            lax.all_gather(norm_gains, "dp", axis=1, tiled=True),
        )

    def fetch_mlp():
        return (
            lax.all_gather(w_gate, "dp", axis=0, tiled=True),
            lax.all_gather(w_up, "dp", axis=0, tiled=True),
            lax.all_gather(w_down, "dp", axis=1, tiled=True),
        )

    def gather_rows(values):
        return lax.all_gather(values, "tensor", axis=0, tiled=True)

    def scatter_rows(values):
        return lax.psum_scatter(values, "tensor", scatter_dimension=0, tiled=True)

    def gather_grads(values):
        return lax.all_gather(values, "tensor", axis=0, tiled=True)

    def scatter_grads(values):
        return lax.psum_scatter(values, "tensor", scatter_dimension=0, tiled=True)

    local_rows = x_input[0].astype(jnp.float32)
    cond_rows = cond_tokens[0]
    mask_float = valid_mask[0].astype(jnp.float32)
    width = local_rows.shape[1]
    token_total = float(lax.axis_size("dp") * lax.axis_size("tensor") * local_rows.shape[0])
    weight_q, weight_k, weight_v, weight_o, cross_q, cross_k, cross_v, cross_o, gains_bf = (
        fetch_attention()
    )
    gains = gains_bf.astype(jnp.float32)
    normed_one, inverse_one = norm_stats(local_rows)
    input_one = gather_rows((normed_one * gains[0]).astype(bf_type))
    length = input_one.shape[0]
    ctx_len = cond_rows.shape[0]
    rot_cos, rot_sin = rotary_tables(length)
    query_rot = rotate(
        matmul(input_one, weight_q).reshape(length, -1, HEAD_DIM), rot_cos, rot_sin
    ).astype(bf_type)
    key_rot = rotate(
        matmul(input_one, weight_k).reshape(length, -1, HEAD_DIM), rot_cos, rot_sin
    ).astype(bf_type)
    value_self = matmul(input_one, weight_v).astype(bf_type).reshape(length, -1, HEAD_DIM)
    mixed_self, log_self = attend_forward(query_rot, key_rot, value_self)
    mixed_self = mixed_self.reshape(length, -1).astype(bf_type)
    hidden_one = local_rows + scatter_rows(matmul(mixed_self, weight_o))
    normed_two, inverse_two = norm_stats(hidden_one)
    input_two = gather_rows((normed_two * gains[1]).astype(bf_type))
    query_cross = matmul(input_two, cross_q).astype(bf_type).reshape(length, -1, HEAD_DIM)
    key_cross = matmul(cond_rows, cross_k).astype(bf_type).reshape(ctx_len, -1, HEAD_DIM)
    value_cross = matmul(cond_rows, cross_v).astype(bf_type).reshape(ctx_len, -1, HEAD_DIM)
    mixed_cross, log_cross = attend_forward(query_cross, key_cross, value_cross)
    mixed_cross = mixed_cross.reshape(length, -1).astype(bf_type)
    hidden_two = hidden_one + scatter_rows(matmul(mixed_cross, cross_o))
    weight_gate, weight_up, weight_down = fetch_mlp()
    normed_three, inverse_three = norm_stats(hidden_two)
    input_three = gather_rows((normed_three * gains[2]).astype(bf_type))
    gate_pre = matmul(input_three, weight_gate)
    up_pre = matmul(input_three, weight_up)
    gate_sigmoid = jax.nn.sigmoid(gate_pre)
    gate_silu = gate_pre * gate_sigmoid
    hidden_ff = (gate_silu * up_pre).astype(bf_type)
    block_out = hidden_two + scatter_rows(matmul(hidden_ff, weight_down))
    error_diff = block_out - teacher[0].astype(jnp.float32)
    local_error = jnp.sum(mask_float[:, None] * error_diff * error_diff)
    valid_count, error_total = lax.psum((jnp.sum(mask_float), local_error), ("dp", "tensor"))
    mean_loss = error_total / (width * valid_count)
    grad_out = 2.0 * token_total / valid_count * mask_float[:, None] * error_diff
    weight_gate, weight_up, weight_down = fetch_mlp()
    branch_three = gather_grads(grad_out.astype(bf_type))
    grad_hidden = times_transposed(branch_three, weight_down)
    grad_down = contract_rows(hidden_ff, branch_three)
    grad_gate = (
        grad_hidden * up_pre * gate_sigmoid * (1.0 + gate_pre * (1.0 - gate_sigmoid))
    ).astype(bf_type)
    grad_upper = (grad_hidden * gate_silu).astype(bf_type)
    grad_gate_w = contract_rows(input_three, grad_gate)
    grad_up_w = contract_rows(input_three, grad_upper)
    grad_normed_three = scatter_grads(
        times_transposed(grad_gate, weight_gate) + times_transposed(grad_upper, weight_up)
    )
    grad_gate_s, grad_up_s, grad_down_s = (
        lax.psum_scatter(grad_gate_w, "dp", scatter_dimension=0, tiled=True),
        lax.psum_scatter(grad_up_w, "dp", scatter_dimension=0, tiled=True),
        lax.psum_scatter(grad_down, "dp", scatter_dimension=1, tiled=True),
    )
    back_three, gain_three = norm_back(grad_normed_three, normed_three, inverse_three, gains[2])
    grad_two = grad_out + back_three
    weight_q, weight_k, weight_v, weight_o, cross_q, cross_k, cross_v, cross_o, spare_gains = (
        fetch_attention()
    )
    branch_two = gather_grads(grad_two.astype(bf_type))
    grad_cross_o = contract_rows(mixed_cross, branch_two)
    grad_mixed_cross = (
        times_transposed(branch_two, cross_o).astype(bf_type).reshape(length, -1, HEAD_DIM)
    )
    grad_qc, grad_kc, grad_vc = attend_back(
        query_cross, key_cross, value_cross, log_cross, grad_mixed_cross
    )
    grad_qc = grad_qc.reshape(length, -1).astype(bf_type)
    grad_kc = grad_kc.reshape(ctx_len, -1).astype(bf_type)
    grad_vc = grad_vc.reshape(ctx_len, -1).astype(bf_type)
    grad_cross_q = contract_rows(input_two, grad_qc)
    grad_cross_k = contract_rows(cond_rows, grad_kc)
    grad_cross_v = contract_rows(cond_rows, grad_vc)
    cond_part = times_transposed(grad_kc, cross_k) + times_transposed(grad_vc, cross_v)
    grad_normed_two = scatter_grads(times_transposed(grad_qc, cross_q))
    back_two, gain_two = norm_back(grad_normed_two, normed_two, inverse_two, gains[1])
    grad_one = grad_two + back_two
    branch_one = gather_grads(grad_one.astype(bf_type))
    grad_self_o = contract_rows(mixed_self, branch_one)
    grad_mixed_self = (
        times_transposed(branch_one, weight_o).astype(bf_type).reshape(length, -1, HEAD_DIM)
    )
    grad_qs, grad_ks, grad_vs = attend_back(
        query_rot, key_rot, value_self, log_self, grad_mixed_self
    )
    grad_qs = rotate_back(grad_qs, rot_cos, rot_sin).reshape(length, -1).astype(bf_type)
    grad_ks = rotate_back(grad_ks, rot_cos, rot_sin).reshape(length, -1).astype(bf_type)
    grad_vs = grad_vs.reshape(length, -1).astype(bf_type)
    grad_self_q = contract_rows(input_one, grad_qs)
    grad_self_k = contract_rows(input_one, grad_ks)
    grad_self_v = contract_rows(input_one, grad_vs)
    grad_normed_one = scatter_grads(
        times_transposed(grad_qs, weight_q)
        + times_transposed(grad_ks, weight_k)
        + times_transposed(grad_vs, weight_v)
    )
    back_one, gain_one = norm_back(grad_normed_one, normed_one, inverse_one, gains[0])
    grad_rows = grad_one + back_one
    gain_part = jnp.stack([gain_one, gain_two, gain_three])
    cond_sum, gain_sum = (
        lax.psum(cond_part.astype(jnp.bfloat16), "tensor").astype(jnp.float32),
        lax.psum(gain_part.astype(jnp.bfloat16), "tensor").astype(jnp.float32),
    )
    (
        grad_q_s,
        grad_k_s,
        grad_v_s,
        grad_o_s,
        grad_cq_s,
        grad_ck_s,
        grad_cv_s,
        grad_co_s,
        grad_gain_s,
    ) = (
        lax.psum_scatter(grad_self_q, "dp", scatter_dimension=0, tiled=True),
        lax.psum_scatter(grad_self_k, "dp", scatter_dimension=0, tiled=True),
        lax.psum_scatter(grad_self_v, "dp", scatter_dimension=0, tiled=True),
        lax.psum_scatter(grad_self_o, "dp", scatter_dimension=1, tiled=True),
        lax.psum_scatter(grad_cross_q, "dp", scatter_dimension=0, tiled=True),
        lax.psum_scatter(grad_cross_k, "dp", scatter_dimension=0, tiled=True),
        lax.psum_scatter(grad_cross_v, "dp", scatter_dimension=0, tiled=True),
        lax.psum_scatter(grad_cross_o, "dp", scatter_dimension=1, tiled=True),
        lax.psum_scatter(gain_sum, "dp", scatter_dimension=1, tiled=True),
    )
    return (
        block_out.astype(bf_type)[None],
        mean_loss,
        grad_rows[None],
        cond_sum[None],
        grad_q_s,
        grad_k_s,
        grad_v_s,
        grad_o_s,
        grad_cq_s,
        grad_ck_s,
        grad_cv_s,
        grad_co_s,
        grad_gate_s,
        grad_up_s,
        grad_down_s,
        grad_gain_s,
    )


def solution(mesh):
    return jax.shard_map(
        body,
        mesh=mesh,
        in_specs=(
            P("dp", "tensor", None),
            P("dp", None, None),
            P("dp", "tensor", None),
            P("dp", "tensor"),
            P(None, "dp"),
            P("dp", "tensor"),
            P("dp", "tensor"),
            P("dp", "tensor"),
            P("tensor", "dp"),
            P("dp", "tensor"),
            P("dp", "tensor"),
            P("dp", "tensor"),
            P("tensor", "dp"),
            P("dp", "tensor"),
            P("dp", "tensor"),
            P("tensor", "dp"),
        ),
        out_specs=(
            P("dp", "tensor", None),
            P(),
            P("dp", "tensor", None),
            P("dp", None, None),
            P("dp", "tensor"),
            P("dp", "tensor"),
            P("dp", "tensor"),
            P("tensor", "dp"),
            P("dp", "tensor"),
            P("dp", "tensor"),
            P("dp", "tensor"),
            P("tensor", "dp"),
            P("dp", "tensor"),
            P("dp", "tensor"),
            P("tensor", "dp"),
            P(None, "dp"),
        ),
        check_vma=False,
    )
```

profile of v0, /device:TPU:0, one launch (start us, length us, event | category | flops | bytes accessed | tf_op | source)
XLA Modules:
  0.0 2735.1 jit_solution(5155967029090758559)
XLA Ops:
  69.5 44.6 %all-gather.25.cloned.1.call-done = bf16[1536,768]{1,0:T(8,128)(2,1)} async-done(((bf16[96,768]{1,0:T(8,128)(2,1)}), bf16[1536,768]{1,0:T(8,128)(2,1)}) %all-gather.25.cloned.1.call-update) | async-done | bytes 2359312 | tf_op jit(solution)/shard_map/all_gather | solution.py:134
  252.2 56.6 %reduce-scatter.25.cloned.1.call-done = f32[384,1536]{1,0:T(8,128)} async-done(((f32[768,1536]{1,0:T(8,128)}), f32[384,1536]{1,0:T(8,128)}) %reduce-scatter.25.cloned.1.call-update) | async-done | bytes 2359312 | tf_op jit(solution)/shard_map/reduce_scatter | solution.py:155
  314.0 39.8 %all-gather.29.cloned.1.call-done = bf16[1536,768]{1,0:T(8,128)(2,1)} async-done(((bf16[96,768]{1,0:T(8,128)(2,1)}), bf16[1536,768]{1,0:T(8,128)(2,1)}) %all-gather.29.cloned.1.call-update) | async-done | bytes 2359312 | tf_op jit(solution)/shard_map/all_gather | solution.py:139
  356.9 40.6 %all-gather.35.cloned.1.call-done = bf16[1536,768]{1,0:T(8,128)(2,1)} async-done(((bf16[96,768]{1,0:T(8,128)(2,1)}), bf16[1536,768]{1,0:T(8,128)(2,1)}) %all-gather.35.cloned.1.call-update) | async-done | bytes 2359312 | tf_op jit(solution)/shard_map/all_gather | solution.py:138
  399.8 41.3 %all-gather.33.cloned.1.call-done = bf16[1536,768]{1,0:T(8,128)(2,1)} async-done(((bf16[96,768]{1,0:T(8,128)(2,1)}), bf16[1536,768]{1,0:T(8,128)(2,1)}) %all-gather.33.cloned.1.call-update) | async-done | bytes 2359312 | tf_op jit(solution)/shard_map/all_gather | solution.py:137
  530.0 58.1 %reduce-scatter.27.cloned.1.call-done = f32[384,1536]{1,0:T(8,128)} async-done(((f32[768,1536]{1,0:T(8,128)}), f32[384,1536]{1,0:T(8,128)}) %reduce-scatter.27.cloned.1.call-update) | async-done | bytes 2359312 | tf_op jit(solution)/shard_map/reduce_scatter | solution.py:155
  594.5 77.3 %all-gather.41.cloned.1.call-done = bf16[1536,3072]{1,0:T(8,128)(2,1)} async-done(((bf16[96,3072]{1,0:T(8,128)(2,1)}), bf16[1536,3072]{1,0:T(8,128)(2,1)}) %all-gather.41.cloned.1.call-update) | async-done | bytes 9437200 | tf_op jit(solution)/shard_map/all_gather | solution.py:146
  722.2 69.5 %all-gather.43.cloned.1.call-done = bf16[1536,3072]{1,0:T(8,128)(2,1)} async-done(((bf16[96,3072]{1,0:T(8,128)(2,1)}), bf16[1536,3072]{1,0:T(8,128)(2,1)}) %all-gather.43.cloned.1.call-update) | async-done | bytes 9437200 | tf_op jit(solution)/shard_map/all_gather | solution.py:147
  808.0 65.4 %all-gather.45.cloned.1.call-done = bf16[3072,1536]{0,1:T(8,128)(2,1)} async-done(((bf16[3072,96]{0,1:T(8,128)(2,1)}), bf16[3072,1536]{0,1:T(8,128)(2,1)}) %all-gather.45.cloned.1.call-update) | async-done | bytes 9437200 | tf_op jit(solution)/shard_map/all_gather | solution.py:148
  887.7 39.0 %psum.29 = f32[]{:T(128)} all-reduce(f32[]{:T(128)} %get-tuple-element.93), channel_id=1, replica_groups=mesh['dp'=16,'tensor'=2] {'dp','tensor'}, use_global_device_ids=true, to_apply=%region_16.0 | all-reduce | flops 1 | bytes 8 | tf_op jit(solution)/shard_map/psum | solution.py:206
  1029.3 60.1 %reduce-scatter.31.cloned.1.call-done = f32[384,1536]{1,0:T(8,128)} async-done(((f32[768,1536]{1,0:T(8,128)}), f32[384,1536]{1,0:T(8,128)}) %reduce-scatter.31.cloned.1.call-update) | async-done | bytes 2359312 | tf_op jit(solution)/shard_map/reduce_scatter | solution.py:161
  1151.6 60.1 %reduce-scatter.33.cloned.1.call-done = f32[384,1536]{1,0:T(8,128)} async-done(((f32[768,1536]{1,0:T(8,128)}), f32[384,1536]{1,0:T(8,128)}) %reduce-scatter.33.cloned.1.call-update) | async-done | bytes 2359312 | tf_op jit(solution)/shard_map/reduce_scatter | solution.py:161
  1356.9 48.8 %reduce-scatter.35.cloned.1.call-done = f32[384,1536]{1,0:T(8,128)} async-done(((f32[768,1536]{1,0:T(8,128)}), f32[384,1536]{1,0:T(8,128)}) %reduce-scatter.35.cloned.1.call-update) | async-done | bytes 2359312 | tf_op jit(solution)/shard_map/reduce_scatter | solution.py:161
  1519.5 42.2 %psum.28 = f32[]{:T(128)} all-reduce(f32[]{:T(128)} %get-tuple-element.89), channel_id=1, replica_groups=mesh['dp'=16,'tensor'=2] {'dp','tensor'}, use_global_device_ids=true, to_apply=%region_14.0 | all-reduce | flops 1 | bytes 8 | tf_op jit(solution)/shard_map/psum | solution.py:206
  1575.0 78.9 %reduce-scatter.45.cloned.1.call-done = f32[96,768]{1,0:T(8,128)} async-done(((f32[1536,768]{1,0:T(8,128)}), f32[96,768]{1,0:T(8,128)}) %reduce-scatter.45.cloned.1.call-update) | async-done | bytes 294928 | tf_op jit(solution)/shard_map/reduce_scatter | solution.py:291
  1653.9 79.6 %reduce-scatter.57.cloned.1.call-done = f32[96,768]{1,0:T(8,128)} async-done(((f32[1536,768]{1,0:T(8,128)}), f32[96,768]{1,0:T(8,128)}) %reduce-scatter.57.cloned.1.call-update) | async-done | bytes 294928
  1733.5 79.1 %reduce-scatter.55.cloned.1.call-done = f32[96,768]{1,0:T(8,128)} async-done(((f32[1536,768]{1,0:T(8,128)}), f32[96,768]{1,0:T(8,128)}) %reduce-scatter.55.cloned.1.call-update) | async-done | bytes 294928
  1812.6 198.9 %reduce-scatter.53.cloned.1.call-done = f32[3072,96]{0,1:T(8,128)} async-done(((f32[3072,1536]{0,1:T(8,128)}), f32[3072,96]{0,1:T(8,128)}) %reduce-scatter.53.cloned.1.call-update) | async-done | bytes 1179664 | tf_op jit(solution)/shard_map/reduce_scatter | solution.py:225
  2011.5 199.2 %reduce-scatter.51.cloned.1.call-done = f32[96,3072]{1,0:T(8,128)} async-done(((f32[1536,3072]{1,0:T(8,128)}), f32[96,3072]{1,0:T(8,128)}) %reduce-scatter.51.cloned.1.call-update) | async-done | bytes 1179664 | tf_op jit(solution)/shard_map/reduce_scatter | solution.py:224
  2210.7 199.3 %reduce-scatter.49.cloned.1.call-done = f32[96,3072]{1,0:T(8,128)} async-done(((f32[1536,3072]{1,0:T(8,128)}), f32[96,3072]{1,0:T(8,128)}) %reduce-scatter.49.cloned.1.call-update) | async-done | bytes 1179664 | tf_op jit(solution)/shard_map/reduce_scatter | solution.py:223
  2410.0 79.5 %reduce-scatter.43.cloned.1.call-done = f32[768,96]{0,1:T(8,128)} async-done(((f32[768,1536]{0,1:T(8,128)}), f32[768,96]{0,1:T(8,128)}) %reduce-scatter.43.cloned.1.call-update) | async-done | bytes 294928 | tf_op jit(solution)/shard_map/reduce_scatter | solution.py:290
  2489.5 79.1 %reduce-scatter.41.cloned.1.call-done = f32[96,768]{1,0:T(8,128)} async-done(((f32[1536,768]{1,0:T(8,128)}), f32[96,768]{1,0:T(8,128)}) %reduce-scatter.41.cloned.1.call-update) | async-done | bytes 294928 | tf_op jit(solution)/shard_map/reduce_scatter | solution.py:289
  2568.5 79.6 %reduce-scatter.39.cloned.1.call-done = f32[96,768]{1,0:T(8,128)} async-done(((f32[1536,768]{1,0:T(8,128)}), f32[96,768]{1,0:T(8,128)}) %reduce-scatter.39.cloned.1.call-update) | async-done | bytes 294928 | tf_op jit(solution)/shard_map/reduce_scatter | solution.py:288
  2648.1 78.9 %reduce-scatter.37.cloned.1.call-done = f32[96,768]{1,0:T(8,128)} async-done(((f32[1536,768]{1,0:T(8,128)}), f32[96,768]{1,0:T(8,128)}) %reduce-scatter.37.cloned.1.call-update) | async-done | bytes 294928 | tf_op jit(solution)/shard_map/reduce_scatter | solution.py:287
  (342 shorter events, 820.7 us)
Async XLA Ops:
  37.4 163.4 %all-gather.21.cloned.1.call-start = ((), (), s32[]{:S(2)}) async-start(), calls=%async_computation.19 | async-start | bytes 2506752 | tf_op jit(solution)/shard_map/all_gather | solution.py:135
  38.0 206.1 %all-gather.27.cloned.1.call-start = ((), (), s32[]{:S(2)}) async-start(), calls=%async_computation.22 | async-start | bytes 2506752 | tf_op jit(solution)/shard_map/all_gather | solution.py:136
  38.6 270.3 %reduce-scatter.25.cloned.1.call-start = ((), (), s32[]{:S(2)}) async-start(), calls=%async_computation.23 | async-start | bytes 7077888 | tf_op jit(solution)/shard_map/reduce_scatter | solution.py:155
  251.5 189.7 %all-gather.33.cloned.1.call-start = ((), (), s32[]{:S(2)}) async-start(), calls=%async_computation.26 | async-start | bytes 2506752 | tf_op jit(solution)/shard_map/all_gather | solution.py:137
  252.2 225.9 %all-gather.31.cloned.1.call-start = ((), (), s32[]{:S(2)}) async-start(), calls=%async_computation.25 | async-start | bytes 3538944 | tf_op jit(solution)/shard_map/all_gather | solution.py:152
  313.0 209.9 %all-gather.37.cloned.1.call-start = ((), (), s32[]{:S(2)}) async-start(), calls=%async_computation.28 | async-start | bytes 2506752 | tf_op jit(solution)/shard_map/all_gather | solution.py:140
  313.8 274.3 %reduce-scatter.27.cloned.1.call-start = ((), (), s32[]{:S(2)}) async-start(), calls=%async_computation.29 | async-start | bytes 7077888 | tf_op jit(solution)/shard_map/reduce_scatter | solution.py:155
  529.9 178.2 %all-gather.39.cloned.1.call-start = ((), (), s32[]{:S(2)}) async-start(), calls=%async_computation.30 | async-start | bytes 3538944 | tf_op jit(solution)/shard_map/all_gather | solution.py:152
  593.1 198.6 %all-gather.43.cloned.1.call-start = ((), (), s32[]{:S(2)}) async-start(), calls=%async_computation.32 | async-start | bytes 10027008 | tf_op jit(solution)/shard_map/all_gather | solution.py:147
  593.7 279.7 %all-gather.45.cloned.1.call-start = ((), (), s32[]{:S(2)}) async-start(), calls=%async_computation.33 | async-start | bytes 10027008 | tf_op jit(solution)/shard_map/all_gather | solution.py:148
  594.3 351.8 %reduce-scatter.29.cloned.1.call-start = ((), (), s32[]{:S(2)}) async-start(), calls=%async_computation.34 | async-start | bytes 7077888 | tf_op jit(solution)/shard_map/reduce_scatter | solution.py:155
  1217.5 188.2 %reduce-scatter.35.cloned.1.call-start = ((), (), s32[]{:S(2)}) async-start(), calls=%async_computation.40 | async-start | bytes 7077888 | tf_op jit(solution)/shard_map/reduce_scatter | solution.py:161
  1345.6 216.8 %all-reduce.2.cloned.1.call-start = ((), (), s32[]{:S(2)}) async-start(), calls=%async_computation.41 | async-start | bytes 835584 | tf_op jit(solution)/shard_map/psum | solution.py:273
  1356.9 212.6 %reduce-scatter.59.cloned.1.call-start = ((), (), s32[]{:S(2)}) async-start(), calls=%async_computation.53 | async-start | bytes 835584
  1422.8 231.1 %reduce-scatter.45.cloned.1.call-start = ((), (), s32[]{:S(2)}) async-start(), calls=%async_computation.46 | async-start | bytes 5013504 | tf_op jit(solution)/shard_map/reduce_scatter | solution.py:291
  1429.0 304.5 %reduce-scatter.57.cloned.1.call-start = ((), (), s32[]{:S(2)}) async-start(), calls=%async_computation.52 | async-start | bytes 5013504
  1438.0 374.6 %reduce-scatter.55.cloned.1.call-start = ((), (), s32[]{:S(2)}) async-start(), calls=%async_computation.51 | async-start | bytes 5013504
  1447.3 564.2 %reduce-scatter.53.cloned.1.call-start = ((), (), s32[]{:S(2)}) async-start(), calls=%async_computation.50 | async-start | bytes 20054016 | tf_op jit(solution)/shard_map/reduce_scatter | solution.py:225
  1461.8 748.9 %reduce-scatter.51.cloned.1.call-start = ((), (), s32[]{:S(2)}) async-start(), calls=%async_computation.49 | async-start | bytes 20054016 | tf_op jit(solution)/shard_map/reduce_scatter | solution.py:224
  1475.7 934.3 %reduce-scatter.49.cloned.1.call-start = ((), (), s32[]{:S(2)}) async-start(), calls=%async_computation.48 | async-start | bytes 20054016 | tf_op jit(solution)/shard_map/reduce_scatter | solution.py:223
  1489.7 999.8 %reduce-scatter.43.cloned.1.call-start = ((), (), s32[]{:S(2)}) async-start(), calls=%async_computation.45 | async-start | bytes 5013504 | tf_op jit(solution)/shard_map/reduce_scatter | solution.py:290
  1497.0 1071.5 %reduce-scatter.41.cloned.1.call-start = ((), (), s32[]{:S(2)}) async-start(), calls=%async_computation.44 | async-start | bytes 5013504 | tf_op jit(solution)/shard_map/reduce_scatter | solution.py:289
  1504.2 1143.9 %reduce-scatter.39.cloned.1.call-start = ((), (), s32[]{:S(2)}) async-start(), calls=%async_computation.43 | async-start | bytes 5013504 | tf_op jit(solution)/shard_map/reduce_scatter | solution.py:288
  1511.5 1215.5 %reduce-scatter.37.cloned.1.call-start = ((), (), s32[]{:S(2)}) async-start(), calls=%async_computation.42 | async-start | bytes 5013504 | tf_op jit(solution)/shard_map/reduce_scatter | solution.py:287
  (88 other events, 3885.3 us)
Sparse Core Ops, SparseCore 0:
  71.7 42.3 all-gather.24
  250.1 58.7 reduce-scatter.24
  311.4 42.3 all-gather.28
  480.6 42.3 all-gather.36
  529.3 58.7 reduce-scatter.26
  590.4 81.4 all-gather.40
  710.2 81.4 all-gather.42
  793.8 79.5 all-gather.44
  886.5 59.5 reduce-scatter.28
  1029.4 59.9 reduce-scatter.30
  1151.6 59.9 reduce-scatter.32
  1345.7 59.9 reduce-scatter.34
  1438.3 56.7 reduce-scatter.58
  1499.8 75.1 reduce-scatter.46
  1579.3 74.5 reduce-scatter.44
  1658.8 74.6 reduce-scatter.56
  1737.9 74.6 reduce-scatter.54
  1817.7 193.8 reduce-scatter.52
  2016.8 193.8 reduce-scatter.50
  2215.9 194.0 reduce-scatter.48
  2414.8 74.6 reduce-scatter.42
  2493.9 74.5 reduce-scatter.40
  2573.5 74.5 reduce-scatter.38
  2652.4 74.5 reduce-scatter.36
  (12 shorter events, 441.5 us)
where the time goes:
time: 2740 us
  waiting for transfers between devices  2170 us (79%)
  matrix products  319 us (12%)
  blocking collectives  111 us (4%)
  other arithmetic  78.4 us (3%)
  local copies, waits for them, and re-layouts  35.4 us (1%)
    reduce_scatter x1, waiting for transfers between devices, body(): lax.psum_scatter(grad_gate_w, 'dp', scatter_dimension=0, tiled=True)  199 us
    reduce_scatter x1, waiting for transfers between devices, body(): lax.psum_scatter(grad_up_w, 'dp', scatter_dimension=0, tiled=True)  199 us
    reduce_scatter x1, waiting for transfers between devices, body(): lax.psum_scatter(grad_down, 'dp', scatter_dimension=1, tiled=True)  199 us
    reduce_scatter x3, waiting for transfers between devices, scatter_grads(): return lax.psum_scatter(values, 'tensor', scatter_dimension=0, tiled=True)  169 us
    unnamed x39, waiting for transfers between devices  166 us
    reduce_scatter x3, waiting for transfers between devices, scatter_rows(): return lax.psum_scatter(values, 'tensor', scatter_dimension=0, tiled=True)  133 us
    all_gather x3, waiting for transfers between devices, gather_grads(): return lax.all_gather(values, 'tensor', axis=0, tiled=True)  107 us
    all_gather x3, waiting for transfers between devices, gather_rows(): return lax.all_gather(values, 'tensor', axis=0, tiled=True)  103 us
  transfers between devices with their start and end apart: 36, of which 34 were waited for; matrix products, arithmetic and copies ran while one was open for 8% of the time, Pallas kernels for 0%

commit v1 on v0

--- a/solution.py
+++ b/solution.py
@@ -6,6 +6,11 @@
 
 HEAD_DIM = 64
 EPSILON = 1e-05
+
+
+def axis_by_axis(value, first, second):
+    partial = lax.psum(value, first)
+    return lax.psum(partial, second)
 
 
 def matmul(left_side, right_side):
@@ -203,7 +208,7 @@
     block_out = hidden_two + scatter_rows(matmul(hidden_ff, weight_down))
     error_diff = block_out - teacher[0].astype(jnp.float32)
     local_error = jnp.sum(mask_float[:, None] * error_diff * error_diff)
-    valid_count, error_total = lax.psum((jnp.sum(mask_float), local_error), ("dp", "tensor"))
+    valid_count, error_total = axis_by_axis((jnp.sum(mask_float), local_error), "tensor", "dp")
     mean_loss = error_total / (width * valid_count)
     grad_out = 2.0 * token_total / valid_count * mask_float[:, None] * error_diff
     weight_gate, weight_up, weight_down = fetch_mlp()

time: 2740 us -> 2740 us (level)
    psum x2 -> x4, blocking collectives: 81.2 us -> 73.2 us  [the longest x2 62.1 us: axis_by_axis(): return lax.psum(partial, second)]
where the time goes in v1:
time: 2740 us; the launch traced here: 2730 us
  waiting for transfers between devices  2180 us (80%)
  matrix products  319 us (12%)
  blocking collectives  103 us (4%)
  other arithmetic  78.3 us (3%)
  local copies, waits for them, and re-layouts  35.4 us (1%)
    reduce_scatter x1, waiting for transfers between devices, body(): lax.psum_scatter(grad_gate_w, 'dp', scatter_dimension=0, tiled=True)  199 us
    reduce_scatter x1, waiting for transfers between devices, body(): lax.psum_scatter(grad_down, 'dp', scatter_dimension=1, tiled=True)  199 us
    reduce_scatter x1, waiting for transfers between devices, body(): lax.psum_scatter(grad_up_w, 'dp', scatter_dimension=0, tiled=True)  199 us
    reduce_scatter x3, waiting for transfers between devices, scatter_grads(): return lax.psum_scatter(values, 'tensor', scatter_dimension=0, tiled=True)  169 us
    unnamed x39, waiting for transfers between devices  166 us
    reduce_scatter x3, waiting for transfers between devices, scatter_rows(): return lax.psum_scatter(values, 'tensor', scatter_dimension=0, tiled=True)  135 us
    all_gather x3, waiting for transfers between devices, gather_grads(): return lax.all_gather(values, 'tensor', axis=0, tiled=True)  108 us
    all_gather x3, waiting for transfers between devices, gather_rows(): return lax.all_gather(values, 'tensor', axis=0, tiled=True)  103 us
  transfers between devices with their start and end apart: 36, of which 34 were waited for; matrix products, arithmetic and copies ran while one was open for 8% of the time, Pallas kernels for 0%

profile of v1, /device:TPU:0, one launch (start us, length us, event | category | flops | bytes accessed | tf_op | source)
XLA Modules:
  0.0 2733.9 jit_solution(10189647838008856258)
XLA Ops:
  69.5 44.6 %all-gather.25.cloned.1.call-done = bf16[1536,768]{1,0:T(8,128)(2,1)} async-done(((bf16[96,768]{1,0:T(8,128)(2,1)}), bf16[1536,768]{1,0:T(8,128)(2,1)}) %all-gather.25.cloned.1.call-update) | async-done | bytes 2359312 | tf_op jit(solution)/shard_map/all_gather | solution.py:139
  118.6 38.9 %all-gather.23.cloned.1.call-done = bf16[1536,768]{1,0:T(8,128)(2,1)} async-done(((bf16[96,768]{1,0:T(8,128)(2,1)}), bf16[1536,768]{1,0:T(8,128)(2,1)}) %all-gather.23.cloned.1.call-update) | async-done | bytes 2359312 | tf_op jit(solution)/shard_map/all_gather | solution.py:138
  252.2 56.6 %reduce-scatter.25.cloned.1.call-done = f32[384,1536]{1,0:T(8,128)} async-done(((f32[768,1536]{1,0:T(8,128)}), f32[384,1536]{1,0:T(8,128)}) %reduce-scatter.25.cloned.1.call-update) | async-done | bytes 2359312 | tf_op jit(solution)/shard_map/reduce_scatter | solution.py:160
  314.0 39.8 %all-gather.29.cloned.1.call-done = bf16[1536,768]{1,0:T(8,128)(2,1)} async-done(((bf16[96,768]{1,0:T(8,128)(2,1)}), bf16[1536,768]{1,0:T(8,128)(2,1)}) %all-gather.29.cloned.1.call-update) | async-done | bytes 2359312 | tf_op jit(solution)/shard_map/all_gather | solution.py:144
  356.9 40.6 %all-gather.35.cloned.1.call-done = bf16[1536,768]{1,0:T(8,128)(2,1)} async-done(((bf16[96,768]{1,0:T(8,128)(2,1)}), bf16[1536,768]{1,0:T(8,128)(2,1)}) %all-gather.35.cloned.1.call-update) | async-done | bytes 2359312 | tf_op jit(solution)/shard_map/all_gather | solution.py:143
  399.8 41.3 %all-gather.33.cloned.1.call-done = bf16[1536,768]{1,0:T(8,128)(2,1)} async-done(((bf16[96,768]{1,0:T(8,128)(2,1)}), bf16[1536,768]{1,0:T(8,128)(2,1)}) %all-gather.33.cloned.1.call-update) | async-done | bytes 2359312 | tf_op jit(solution)/shard_map/all_gather | solution.py:142
  441.1 36.9 %all-gather.31.cloned.1.call-done = bf16[768,1536]{1,0:T(8,128)(2,1)} async-done(((bf16[384,1536]{1,0:T(8,128)(2,1)}), bf16[768,1536]{1,0:T(8,128)(2,1)}) %all-gather.31.cloned.1.call-update) | async-done | bytes 2359312 | tf_op jit(solution)/shard_map/all_gather | solution.py:157
  530.0 58.1 %reduce-scatter.27.cloned.1.call-done = f32[384,1536]{1,0:T(8,128)} async-done(((f32[768,1536]{1,0:T(8,128)}), f32[384,1536]{1,0:T(8,128)}) %reduce-scatter.27.cloned.1.call-update) | async-done | bytes 2359312 | tf_op jit(solution)/shard_map/reduce_scatter | solution.py:160
  594.5 77.3 %all-gather.41.cloned.1.call-done = bf16[1536,3072]{1,0:T(8,128)(2,1)} async-done(((bf16[96,3072]{1,0:T(8,128)(2,1)}), bf16[1536,3072]{1,0:T(8,128)(2,1)}) %all-gather.41.cloned.1.call-update) | async-done | bytes 9437200 | tf_op jit(solution)/shard_map/all_gather | solution.py:151
  722.1 69.6 %all-gather.43.cloned.1.call-done = bf16[1536,3072]{1,0:T(8,128)(2,1)} async-done(((bf16[96,3072]{1,0:T(8,128)(2,1)}), bf16[1536,3072]{1,0:T(8,128)(2,1)}) %all-gather.43.cloned.1.call-update) | async-done | bytes 9437200 | tf_op jit(solution)/shard_map/all_gather | solution.py:152
  808.0 65.4 %all-gather.45.cloned.1.call-done = bf16[3072,1536]{0,1:T(8,128)(2,1)} async-done(((bf16[3072,96]{0,1:T(8,128)(2,1)}), bf16[3072,1536]{0,1:T(8,128)(2,1)}) %all-gather.45.cloned.1.call-update) | async-done | bytes 9437200 | tf_op jit(solution)/shard_map/all_gather | solution.py:153
  1028.1 60.1 %reduce-scatter.31.cloned.1.call-done = f32[384,1536]{1,0:T(8,128)} async-done(((f32[768,1536]{1,0:T(8,128)}), f32[384,1536]{1,0:T(8,128)}) %reduce-scatter.31.cloned.1.call-update) | async-done | bytes 2359312 | tf_op jit(solution)/shard_map/reduce_scatter | solution.py:166
  1150.3 60.1 %reduce-scatter.33.cloned.1.call-done = f32[384,1536]{1,0:T(8,128)} async-done(((f32[768,1536]{1,0:T(8,128)}), f32[384,1536]{1,0:T(8,128)}) %reduce-scatter.33.cloned.1.call-update) | async-done | bytes 2359312 | tf_op jit(solution)/shard_map/reduce_scatter | solution.py:166
  1355.7 48.8 %reduce-scatter.35.cloned.1.call-done = f32[384,1536]{1,0:T(8,128)} async-done(((f32[768,1536]{1,0:T(8,128)}), f32[384,1536]{1,0:T(8,128)}) %reduce-scatter.35.cloned.1.call-update) | async-done | bytes 2359312 | tf_op jit(solution)/shard_map/reduce_scatter | solution.py:166
  1573.7 78.9 %reduce-scatter.45.cloned.1.call-done = f32[96,768]{1,0:T(8,128)} async-done(((f32[1536,768]{1,0:T(8,128)}), f32[96,768]{1,0:T(8,128)}) %reduce-scatter.45.cloned.1.call-update) | async-done | bytes 294928 | tf_op jit(solution)/shard_map/reduce_scatter | solution.py:296
  1652.6 79.6 %reduce-scatter.57.cloned.1.call-done = f32[96,768]{1,0:T(8,128)} async-done(((f32[1536,768]{1,0:T(8,128)}), f32[96,768]{1,0:T(8,128)}) %reduce-scatter.57.cloned.1.call-update) | async-done | bytes 294928
  1732.2 79.1 %reduce-scatter.55.cloned.1.call-done = f32[96,768]{1,0:T(8,128)} async-done(((f32[1536,768]{1,0:T(8,128)}), f32[96,768]{1,0:T(8,128)}) %reduce-scatter.55.cloned.1.call-update) | async-done | bytes 294928
  1811.2 199.1 %reduce-scatter.53.cloned.1.call-done = f32[3072,96]{0,1:T(8,128)} async-done(((f32[3072,1536]{0,1:T(8,128)}), f32[3072,96]{0,1:T(8,128)}) %reduce-scatter.53.cloned.1.call-update) | async-done | bytes 1179664 | tf_op jit(solution)/shard_map/reduce_scatter | solution.py:230
  2010.4 199.1 %reduce-scatter.51.cloned.1.call-done = f32[96,3072]{1,0:T(8,128)} async-done(((f32[1536,3072]{1,0:T(8,128)}), f32[96,3072]{1,0:T(8,128)}) %reduce-scatter.51.cloned.1.call-update) | async-done | bytes 1179664 | tf_op jit(solution)/shard_map/reduce_scatter | solution.py:229
  2209.5 199.3 %reduce-scatter.49.cloned.1.call-done = f32[96,3072]{1,0:T(8,128)} async-done(((f32[1536,3072]{1,0:T(8,128)}), f32[96,3072]{1,0:T(8,128)}) %reduce-scatter.49.cloned.1.call-update) | async-done | bytes 1179664 | tf_op jit(solution)/shard_map/reduce_scatter | solution.py:228
  2408.8 79.5 %reduce-scatter.43.cloned.1.call-done = f32[768,96]{0,1:T(8,128)} async-done(((f32[768,1536]{0,1:T(8,128)}), f32[768,96]{0,1:T(8,128)}) %reduce-scatter.43.cloned.1.call-update) | async-done | bytes 294928 | tf_op jit(solution)/shard_map/reduce_scatter | solution.py:295
  2488.3 79.1 %reduce-scatter.41.cloned.1.call-done = f32[96,768]{1,0:T(8,128)} async-done(((f32[1536,768]{1,0:T(8,128)}), f32[96,768]{1,0:T(8,128)}) %reduce-scatter.41.cloned.1.call-update) | async-done | bytes 294928 | tf_op jit(solution)/shard_map/reduce_scatter | solution.py:294
  2567.3 79.6 %reduce-scatter.39.cloned.1.call-done = f32[96,768]{1,0:T(8,128)} async-done(((f32[1536,768]{1,0:T(8,128)}), f32[96,768]{1,0:T(8,128)}) %reduce-scatter.39.cloned.1.call-update) | async-done | bytes 294928 | tf_op jit(solution)/shard_map/reduce_scatter | solution.py:293
  2646.9 78.9 %reduce-scatter.37.cloned.1.call-done = f32[96,768]{1,0:T(8,128)} async-done(((f32[1536,768]{1,0:T(8,128)}), f32[96,768]{1,0:T(8,128)}) %reduce-scatter.37.cloned.1.call-update) | async-done | bytes 294928 | tf_op jit(solution)/shard_map/reduce_scatter | solution.py:292
  (344 shorter events, 824.7 us)
Async XLA Ops:
  37.4 163.4 %all-gather.21.cloned.1.call-start = ((), (), s32[]{:S(2)}) async-start(), calls=%async_computation.19 | async-start | bytes 2506752 | tf_op jit(solution)/shard_map/all_gather | solution.py:140
  38.0 206.1 %all-gather.27.cloned.1.call-start = ((), (), s32[]{:S(2)}) async-start(), calls=%async_computation.22 | async-start | bytes 2506752 | tf_op jit(solution)/shard_map/all_gather | solution.py:141
  38.6 270.3 %reduce-scatter.25.cloned.1.call-start = ((), (), s32[]{:S(2)}) async-start(), calls=%async_computation.23 | async-start | bytes 7077888 | tf_op jit(solution)/shard_map/reduce_scatter | solution.py:160
  251.4 189.7 %all-gather.33.cloned.1.call-start = ((), (), s32[]{:S(2)}) async-start(), calls=%async_computation.26 | async-start | bytes 2506752 | tf_op jit(solution)/shard_map/all_gather | solution.py:142
  252.2 225.9 %all-gather.31.cloned.1.call-start = ((), (), s32[]{:S(2)}) async-start(), calls=%async_computation.25 | async-start | bytes 3538944 | tf_op jit(solution)/shard_map/all_gather | solution.py:157
  313.0 209.9 %all-gather.37.cloned.1.call-start = ((), (), s32[]{:S(2)}) async-start(), calls=%async_computation.28 | async-start | bytes 2506752 | tf_op jit(solution)/shard_map/all_gather | solution.py:145
  313.7 274.3 %reduce-scatter.27.cloned.1.call-start = ((), (), s32[]{:S(2)}) async-start(), calls=%async_computation.29 | async-start | bytes 7077888 | tf_op jit(solution)/shard_map/reduce_scatter | solution.py:160
  529.9 178.2 %all-gather.39.cloned.1.call-start = ((), (), s32[]{:S(2)}) async-start(), calls=%async_computation.30 | async-start | bytes 3538944 | tf_op jit(solution)/shard_map/all_gather | solution.py:157
  593.1 198.6 %all-gather.43.cloned.1.call-start = ((), (), s32[]{:S(2)}) async-start(), calls=%async_computation.32 | async-start | bytes 10027008 | tf_op jit(solution)/shard_map/all_gather | solution.py:152
  593.7 279.7 %all-gather.45.cloned.1.call-start = ((), (), s32[]{:S(2)}) async-start(), calls=%async_computation.33 | async-start | bytes 10027008 | tf_op jit(solution)/shard_map/all_gather | solution.py:153
  594.3 350.5 %reduce-scatter.29.cloned.1.call-start = ((), (), s32[]{:S(2)}) async-start(), calls=%async_computation.34 | async-start | bytes 7077888 | tf_op jit(solution)/shard_map/reduce_scatter | solution.py:160
  1216.2 188.2 %reduce-scatter.35.cloned.1.call-start = ((), (), s32[]{:S(2)}) async-start(), calls=%async_computation.40 | async-start | bytes 7077888 | tf_op jit(solution)/shard_map/reduce_scatter | solution.py:166
  1344.3 211.9 %all-reduce.2.cloned.1.call-start = ((), (), s32[]{:S(2)}) async-start(), calls=%async_computation.41 | async-start | bytes 835584 | tf_op jit(solution)/shard_map/psum | solution.py:278
  1355.6 207.7 %reduce-scatter.59.cloned.1.call-start = ((), (), s32[]{:S(2)}) async-start(), calls=%async_computation.53 | async-start | bytes 835584
  1421.5 231.1 %reduce-scatter.45.cloned.1.call-start = ((), (), s32[]{:S(2)}) async-start(), calls=%async_computation.46 | async-start | bytes 5013504 | tf_op jit(solution)/shard_map/reduce_scatter | solution.py:296
  1427.7 304.4 %reduce-scatter.57.cloned.1.call-start = ((), (), s32[]{:S(2)}) async-start(), calls=%async_computation.52 | async-start | bytes 5013504
  1436.8 374.5 %reduce-scatter.55.cloned.1.call-start = ((), (), s32[]{:S(2)}) async-start(), calls=%async_computation.51 | async-start | bytes 5013504
  1446.0 564.3 %reduce-scatter.53.cloned.1.call-start = ((), (), s32[]{:S(2)}) async-start(), calls=%async_computation.50 | async-start | bytes 20054016 | tf_op jit(solution)/shard_map/reduce_scatter | solution.py:230
  1460.5 749.0 %reduce-scatter.51.cloned.1.call-start = ((), (), s32[]{:S(2)}) async-start(), calls=%async_computation.49 | async-start | bytes 20054016 | tf_op jit(solution)/shard_map/reduce_scatter | solution.py:229
  1474.5 934.3 %reduce-scatter.49.cloned.1.call-start = ((), (), s32[]{:S(2)}) async-start(), calls=%async_computation.48 | async-start | bytes 20054016 | tf_op jit(solution)/shard_map/reduce_scatter | solution.py:228
  1488.4 999.9 %reduce-scatter.43.cloned.1.call-start = ((), (), s32[]{:S(2)}) async-start(), calls=%async_computation.45 | async-start | bytes 5013504 | tf_op jit(solution)/shard_map/reduce_scatter | solution.py:295
  1495.7 1071.6 %reduce-scatter.41.cloned.1.call-start = ((), (), s32[]{:S(2)}) async-start(), calls=%async_computation.44 | async-start | bytes 5013504 | tf_op jit(solution)/shard_map/reduce_scatter | solution.py:294
  1502.9 1144.0 %reduce-scatter.39.cloned.1.call-start = ((), (), s32[]{:S(2)}) async-start(), calls=%async_computation.43 | async-start | bytes 5013504 | tf_op jit(solution)/shard_map/reduce_scatter | solution.py:293
  1510.3 1215.5 %reduce-scatter.37.cloned.1.call-start = ((), (), s32[]{:S(2)}) async-start(), calls=%async_computation.42 | async-start | bytes 5013504 | tf_op jit(solution)/shard_map/reduce_scatter | solution.py:292
  (88 other events, 3882.8 us)
Sparse Core Ops, SparseCore 0:
  71.7 42.3 all-gather.24
  250.0 58.7 reduce-scatter.24
  311.4 42.3 all-gather.28
  480.6 42.3 all-gather.36
  529.3 58.7 reduce-scatter.26
  590.4 81.4 all-gather.40
  710.2 81.4 all-gather.42
  793.8 79.5 all-gather.44
  886.5 58.1 reduce-scatter.28
  1028.2 59.9 reduce-scatter.30
  1150.4 59.9 reduce-scatter.32
  1344.4 59.9 reduce-scatter.34
  1437.0 56.6 reduce-scatter.58
  1498.5 75.1 reduce-scatter.46
  1578.0 74.5 reduce-scatter.44
  1657.5 74.5 reduce-scatter.56
  1736.6 74.5 reduce-scatter.54
  1816.3 193.9 reduce-scatter.52
  2015.6 193.8 reduce-scatter.50
  2214.7 194.0 reduce-scatter.48
  2413.6 74.6 reduce-scatter.42
  2492.7 74.5 reduce-scatter.40
  2572.3 74.5 reduce-scatter.38
  2651.2 74.5 reduce-scatter.36
  (12 shorter events, 441.7 us)
